TPU v7x, 32 devices: a whole 2x2x4 slice. The times are simulated.
32 devices in a mesh: gx: 8 (over z, y), gz: 4 (over x, core).
Axes of the slice: x: 2, y: 2, z: 4, core: 2. Of those that a mesh axis runs over, the one named last changes fastest.
Arguments:
- velocity_field: float32 [3, 3072, 16, 512], P(None, 'gx', None, 'gz'), may hold values from -6 to 6
- interp_weight: bfloat16 [2048, 128, 512], P(('gx', 'gz')), may hold values from -0.25 to 0.25
- particle_velocity: float32 [3, 2048, 128], P(None, ('gx', 'gz')), may hold values from -6 to 6
- tile_owner: int32 [8192, 1], P(('gx', 'gz')), may hold values from 0 to 31; in each aligned block of 256 rows (0 to 255, 256 to 511, ...) at most 24 rows name the same one
- tile_index: int32 [8192], P(('gx', 'gz')), may hold values from 0 to 6143
- block_count: int32 [32], P(('gx', 'gz')), may hold values from 16 to 64, as said below
Outputs:
- fluid_rhs: float32 [3, 3072, 16, 512], P(None, 'gx', None, 'gz')
- new_velocity: float32 [3, 2048, 128], P(None, ('gx', 'gz'))
Inputs may be any that keep to these rules, and one draw needn't show every extreme that they name: `tile_owner`: among the 256 requests of one device, no owner is named more than 24 times, a bound that some block reaches. `block_count`: some device has all 64 blocks live.
All inputs are finite; a program needn't handle non-finite values.
Results may differ from a plain program's by a relative error of at most 0.0014.
Values may be sent and summed in bfloat16 or wider, within the bound.
A program may use at most 256 MiB of HBM per device.

v0:
```python
import functools
import math

import jax
import jax.numpy as jnp
from jax import lax
from jax.experimental import pallas as pl
from jax.experimental.pallas import tpu as pltpu
from jax.sharding import PartitionSpec as P

ROOT = (math.sqrt(5.0) / 3.0 - 1.0) * 1.5
GREEN_GAIN = 3.0 / math.sqrt(5.0)
GAMMA = (25.0 / 36.0) * GREEN_GAIN * (1.0 - ROOT * ROOT)
EPS = (1.0 / 12.0) / GAMMA
VISCOSITY = 0.2
RELAX_TIME = 1.0
TIME_STEP = 0.5
LOADING = 0.5
WINDOW = 96
F32 = jnp.float32
BF16 = jnp.bfloat16
VMEM_LIMIT = 56 * 1024 * 1024


def iota(shape, dim):
    return lax.broadcasted_iota(jnp.int32, shape, dim)


def dot(a, b, ca, cb):
    return lax.dot_general(a, b, (((ca,), (cb,)), ((), ())), preferred_element_type=F32)


def prep_kernel(kt, capacity, owner_ref, index_ref, send_ref, slot_ref):
    count = owner_ref.shape[1]
    devices = send_ref.shape[0]
    blocks = count // kt
    rows, cols = iota((count, count), 0), iota((count, count), 1)
    pick = cols == kt * (rows % blocks) + rows // blocks
    owner = jnp.sum(jnp.where(pick, owner_ref[...], 0), 1, keepdims=True)
    index = jnp.sum(jnp.where(pick, index_ref[...], 0), 1, keepdims=True)
    named = owner == iota((count, devices), 1)
    onehot = named.astype(F32)
    lower = (cols <= rows).astype(F32).astype(BF16)
    seen = dot(lower, onehot.astype(BF16), 1, 0)
    position = jnp.sum(seen * onehot, 1, keepdims=True).astype(jnp.int32) - 1
    slot_ref[...] = owner * capacity + position
    place = position == iota((count, capacity), 1)
    high = jnp.where(place, (index // 128).astype(F32), 0.0).astype(BF16)
    low = jnp.where(place, (index % 128).astype(F32), 0.0).astype(BF16)
    turned = onehot.astype(BF16)
    high_sum, low_sum = dot(turned, high, 0, 0), dot(turned, low, 0, 0)
    send_ref[...] = high_sum.astype(jnp.int32) * 128 + low_sum.astype(jnp.int32)


def row_fields(ref, i):
    u = [ref[c, i] for c in range(3)]
    return u + [u[0] * u[c] for c in range(3)]


def edge_kernel(u_ref, right_ref, left_ref, low_ref, high_ref):
    step, last = pl.program_id(0), pl.num_programs(0) - 1
    window, wall, span = u_ref.shape[1:]
    shape = (8, span)
    pick = jnp.where(
        ((iota(shape, 0) == 0) & (iota(shape, 1) == 0))
        | ((iota(shape, 0) == 1) & (iota(shape, 1) == span - 1)),
        1.0,
        0.0,
    ).astype(BF16)
    for c in range(3):
        cells = u_ref[c].reshape(window * wall, span).astype(BF16)
        lanes = dot(pick, cells, 1, 1)
        low_ref[c] = lanes[0:1].astype(BF16)
        high_ref[c] = lanes[1:2].astype(BF16)

    def body(order):
        def one(i, state):
            fields = row_fields(u_ref, order(i))
            return tuple(f + ROOT * s for f, s in zip(fields, state))

        return lax.fori_loop(0, window, one, (jnp.zeros((wall, span), F32),) * 6, unroll=4)

    @pl.when(step == last)
    def _():
        for k, value in enumerate(body(lambda i: i)):
            right_ref[k] = value
        for c in range(3):
            right_ref[6 + c] = u_ref[c, window - 1]

    @pl.when(step == 0)
    def _():
        for k, value in enumerate(body(lambda i: window - 1 - i)):
            left_ref[k] = value
        for c in range(3):
            left_ref[6 + c] = u_ref[c, 0]


def gather_kernel(index_ref, field_ref, out_ref, rows_ref):
    count = out_ref.shape[0]
    span = field_ref.shape[2]

    def one(r, carry):
        row = index_ref[0, r]
        for c in range(3):
            rows_ref[c, pl.ds(r, 1), :] = field_ref[c, pl.ds(row, 1), :]
        return carry

    lax.fori_loop(0, count, one, 0, unroll=8)
    for c in range(3):
        out_ref[:, c * span : (c + 1) * span] = rows_ref[c].astype(BF16)


def deriv_kernel(u_ref, low_ref, high_ref, left_ref, right_ref, out_ref, state_ref, part_ref, halo_ref):
    step = pl.program_id(0)
    blocks = pl.num_programs(0) // 2
    rows, wall, span = u_ref.shape[1:]
    lane = iota((wall, span), 1)

    def load_state(edge_ref):
        edge = [edge_ref[6 + c] for c in range(3)]
        edge = edge + [edge[0] * edge[c] for c in range(3)]
        for k in range(6):
            state_ref[k] = edge_ref[k]
            state_ref[6 + k] = edge[k]

    @pl.when(step == 0)
    def _():
        load_state(left_ref)

    @pl.when(step == blocks)
    def _():
        load_state(right_ref)

    def advance(i, carry):
        state, before = carry[:6], carry[6:]
        fields = row_fields(u_ref, i)
        parts = [EPS * f + s for f, s in zip(before, state)]
        sums = [parts[3 + c] + fields[0] * parts[c] for c in range(3)]
        moved = [f + ROOT * s for f, s in zip(fields, state)]
        return fields, sums, tuple(moved) + tuple(fields)

    start = tuple(state_ref[k] for k in range(12))

    @pl.when(step < blocks)
    def _():
        shape = (8, rows * wall)
        corner = (8, span)
        pick = jnp.where(
            ((iota(corner, 0) == 0) & (iota(corner, 1) == 0))
            | ((iota(corner, 0) == 1) & (iota(corner, 1) == span - 1)),
            VISCOSITY,
            0.0,
        )
        for c in range(3):
            ends = jnp.where(
                iota(shape, 0) == 0,
                low_ref[c].astype(F32),
                jnp.where(iota(shape, 0) == 1, high_ref[c].astype(F32), 0.0),
            )
            halo_ref[c] = dot(ends, pick.astype(F32) / VISCOSITY, 0, 0).reshape(rows, wall, span)

        def one(i, carry):
            fields, sums, carry = advance(i, carry)
            for c in range(3):
                u = fields[c]
                near = jnp.where(lane == 0, 0.0, pltpu.roll(u, 1, 1))
                far = jnp.where(lane == span - 1, 0.0, pltpu.roll(u, span - 1, 1))
                curve = near + far + halo_ref[c, i] - 2.0 * u
                part_ref[c, step * rows + i] = 0.5 * GAMMA * sums[c] + VISCOSITY * curve
            return carry

        end = lax.fori_loop(0, rows, one, start, unroll=4)
        for k in range(12):
            state_ref[k] = end[k]

    @pl.when(step >= blocks)
    def _():
        block = 2 * blocks - 1 - step

        def one(n, carry):
            i = rows - 1 - n
            _, sums, carry = advance(i, carry)
            for c in range(3):
                out_ref[c, i] = part_ref[c, block * rows + i] - 0.5 * GAMMA * sums[c]
            return carry

        end = lax.fori_loop(0, rows, one, start, unroll=4)
        for k in range(12):
            state_ref[k] = end[k]


def particle_kernel(kt, live_ref, slot_ref, reply_ref, weight_ref, velocity_ref, moved_ref, out_ref, own_ref, push_ref):
    step, last = pl.program_id(0), pl.num_programs(0) - 1
    group, particles, cells = weight_ref.shape
    count, slots = slot_ref.shape[0], reply_ref.shape[0]
    span = cells // kt
    blocks = count // kt

    @pl.when(step == 0)
    def _():
        chosen = jnp.where(slot_ref[...] == iota((count, slots), 1), 1.0, 0.0).astype(BF16)
        own = dot(chosen, reply_ref[...], 1, 0)
        for j in range(kt):
            for c in range(3):
                own_ref[c, :, j * span : (j + 1) * span] = own[
                    j * blocks : (j + 1) * blocks, c * span : (c + 1) * span
                ]

    base = pl.multiple_of(step * group, group)
    tiles = jnp.concatenate([own_ref[c, pl.ds(base, group), :] for c in range(3)], 0).astype(BF16)
    row = iota((3 * group, particles), 0) % group
    sampled = jnp.zeros((3 * group, particles), F32)
    for b in range(group):
        sampled = jnp.where(row == b, dot(tiles, weight_ref[b], 1, 1), sampled)
    velocity = velocity_ref[...].reshape(3 * group, particles)
    live = jnp.where(row + base < live_ref[0], 1.0, 0.0)
    drag = live * (sampled - velocity) * (1.0 / RELAX_TIME)
    moved_ref[...] = (velocity + TIME_STEP * drag).reshape(3, group, particles)
    half = drag.astype(BF16)
    row = iota((3 * group, cells), 0) % group
    push = jnp.zeros((3 * group, cells), F32)
    for b in range(group):
        push = jnp.where(row == b, dot(half, weight_ref[b], 1, 0), push)
    push = -LOADING * push
    for j in range(kt):
        for c in range(3):
            push_ref[pl.ds(j * blocks + base, group), c * span : (c + 1) * span] = push[
                c * group : (c + 1) * group, j * span : (j + 1) * span
            ]

    @pl.when(step == last)
    def _():
        same = iota((count, count), 0) == iota((count, count), 1)
        slot_row = jnp.sum(jnp.where(same, slot_ref[...], 0), 0, keepdims=True)
        placed = jnp.where(iota((slots, count), 0) == slot_row, 1.0, 0.0).astype(BF16)
        out_ref[...] = dot(placed, push_ref[...].astype(BF16), 1, 0).astype(BF16)


def add_kernel(index_ref, base_ref, back_ref, out_ref):
    rows, span = base_ref.shape[1:]
    slots = back_ref.shape[0]
    ids = iota((rows, slots), 0) + pl.program_id(0) * rows
    named = jnp.where(ids == index_ref[...], 1.0, 0.0).astype(BF16)
    total = dot(named, back_ref[...], 1, 0)
    for c in range(3):
        out_ref[c] = base_ref[c] + total[:, c * span : (c + 1) * span]


def vmem():
    return pl.BlockSpec(memory_space=pltpu.VMEM)


def smem():
    return pl.BlockSpec(memory_space=pltpu.SMEM)


def params():
    return pltpu.CompilerParams(vmem_limit_bytes=VMEM_LIMIT)


def cost(flops, nbytes):
    return pl.CostEstimate(flops=int(flops), bytes_accessed=int(nbytes), transcendentals=0)


def largest_divisor(total, limit):
    return max(d for d in range(1, limit + 1) if total % d == 0)


def shards(velocity_field, interp_weight, particle_velocity, tile_owner, tile_index, block_count):
    _, slab, wall, span = velocity_field.shape
    shape = jax.ShapeDtypeStruct
    gx, gz = lax.axis_size("gx"), lax.axis_size("gz")
    devices = gx * gz
    requests = tile_index.shape[0]
    blocks, particles, cells = interp_weight.shape
    kt = requests // blocks
    capacity = max(2, 3 * requests // devices)
    slots = devices * capacity
    field_bytes = velocity_field.size * 4

    send_index, slot_ids = pl.pallas_call(
        functools.partial(prep_kernel, kt, capacity),
        out_shape=(shape((devices, capacity), jnp.int32), shape((requests, 1), jnp.int32)),
        in_specs=[vmem(), vmem()],
        out_specs=(vmem(), vmem()),
        cost_estimate=cost(1e7, 1e5),
        name="prep",
    )(tile_owner.reshape(1, requests), tile_index.reshape(1, requests))
    got = lax.all_to_all(send_index, ("gx", "gz"), split_axis=0, concat_axis=0, tiled=True)
    got = got.reshape(1, slots)

    window = WINDOW if slab % WINDOW == 0 else slab
    lines = slab * wall
    to_right, to_left, low, high = pl.pallas_call(
        edge_kernel,
        grid=(slab // window,),
        out_shape=(shape((9, wall, span), F32),) * 2 + (shape((3, 1, lines), BF16),) * 2,
        in_specs=[pl.BlockSpec((3, window, wall, span), lambda i: (0, i, 0, 0))],
        out_specs=(pl.BlockSpec((9, wall, span), lambda i: (0, 0, 0)),) * 2
        + (pl.BlockSpec((3, 1, window * wall), lambda i: (0, 0, i)),) * 2,
        compiler_params=params(),
        cost_estimate=cost(1e7, field_bytes),
        name="edges",
    )(velocity_field)
    ahead = lambda n: [(i, (i + 1) % n) for i in range(n)]
    behind = lambda n: [((i + 1) % n, i) for i in range(n)]
    from_left = lax.ppermute(to_right, "gx", ahead(gx))
    from_right = lax.ppermute(to_left, "gx", behind(gx))
    from_low = lax.ppermute(high, "gz", ahead(gz))
    from_high = lax.ppermute(low, "gz", behind(gz))

    tile_data = pl.pallas_call(
        gather_kernel,
        out_shape=shape((slots, 3 * span), BF16),
        in_specs=[smem(), vmem()],
        out_specs=vmem(),
        scratch_shapes=[pltpu.VMEM((3, slots, span), F32)],
        compiler_params=params(),
        cost_estimate=cost(1e6, field_bytes),
        name="gather",
    )(got, velocity_field.reshape(3, lines, span))
    replies = lax.all_to_all(tile_data, ("gx", "gz"), split_axis=0, concat_axis=0, tiled=True)

    rows = largest_divisor(slab, 48)
    parts = slab // rows
    fluid = pl.pallas_call(
        deriv_kernel,
        grid=(2 * parts,),
        out_shape=shape(velocity_field.shape, F32),
        in_specs=[
            pl.BlockSpec((3, rows, wall, span), lambda i: (0, jnp.minimum(i, 2 * parts - 1 - i), 0, 0)),
            pl.BlockSpec((3, 1, rows * wall), lambda i: (0, 0, jnp.minimum(i, parts - 1))),
            pl.BlockSpec((3, 1, rows * wall), lambda i: (0, 0, jnp.minimum(i, parts - 1))),
            pl.BlockSpec((9, wall, span), lambda i: (0, 0, 0)),
            pl.BlockSpec((9, wall, span), lambda i: (0, 0, 0)),
        ],
        out_specs=pl.BlockSpec(
            (3, rows, wall, span), lambda i: (0, jnp.minimum(parts - 1, 2 * parts - 1 - i), 0, 0)
        ),
        scratch_shapes=[
            pltpu.VMEM((12, wall, span), F32),
            pltpu.VMEM((3, slab, wall, span), F32),
            pltpu.VMEM((3, rows, wall, span), F32),
        ],
        compiler_params=params(),
        cost_estimate=cost(velocity_field.size * 40, field_bytes * 3),
        name="deriv",
    )(velocity_field, from_low, from_high, from_left, from_right)

    group = 8
    moved, outgoing = pl.pallas_call(
        functools.partial(particle_kernel, kt),
        grid=(blocks // group,),
        out_shape=(shape(particle_velocity.shape, F32), shape((slots, 3 * span), BF16)),
        in_specs=[
            smem(),
            pl.BlockSpec((requests, 1), lambda i: (0, 0)),
            pl.BlockSpec((slots, 3 * span), lambda i: (0, 0)),
            pl.BlockSpec((group, particles, cells), lambda i: (i, 0, 0)),
            pl.BlockSpec((3, group, particles), lambda i: (0, i, 0)),
        ],
        out_specs=(
            pl.BlockSpec((3, group, particles), lambda i: (0, i, 0)),
            pl.BlockSpec((slots, 3 * span), lambda i: (0, 0)),
        ),
        scratch_shapes=[
            pltpu.VMEM((3, blocks, cells), F32),
            pltpu.VMEM((requests, 3 * span), F32),
        ],
        compiler_params=params(),
        cost_estimate=cost(4e8, interp_weight.size * 2),
        name="particles",
    )(block_count, slot_ids, replies, interp_weight, particle_velocity)
    returned = lax.all_to_all(outgoing, ("gx", "gz"), split_axis=0, concat_axis=0, tiled=True)

    chunk = largest_divisor(lines, 512)
    result = pl.pallas_call(
        add_kernel,
        grid=(lines // chunk,),
        out_shape=shape((3, lines, span), F32),
        in_specs=[
            pl.BlockSpec((1, slots), lambda i: (0, 0)),
            pl.BlockSpec((3, chunk, span), lambda i: (0, i, 0)),
            pl.BlockSpec((slots, 3 * span), lambda i: (0, 0)),
        ],
        out_specs=pl.BlockSpec((3, chunk, span), lambda i: (0, i, 0)),
        compiler_params=params(),
        cost_estimate=cost(2.0 * lines * slots * 3 * span, field_bytes * 2),
        name="feedback",
    )(got, fluid.reshape(3, lines, span), returned)
    return (result.reshape(velocity_field.shape), moved)


def solution(mesh):
    placed = (
        P(None, "gx", None, "gz"),
        P(("gx", "gz"), None, None),
        P(None, ("gx", "gz"), None),
        P(("gx", "gz"), None),
        P(("gx", "gz")),
        P(("gx", "gz")),
    )
    return jax.shard_map(
        shards,
        mesh=mesh,
        in_specs=placed,
        out_specs=(P(None, "gx", None, "gz"), P(None, ("gx", "gz"), None)),
        check_vma=False,
    )
```

profile of v0, /device:TPU:0, one launch (start us, length us, event | category | flops | bytes accessed | tf_op | source)
XLA Modules:
  0.0 119.8 jit_solution(17697431061499957005)
XLA Ops:
  0.6 1.9 %prep.1 = (s32[32,24]{1,0:T(8,128)}, s32[256,1]{1,0:T(8,128)}) custom-call(s32[1,256]{1,0:T(1,128)} %bitcast.20, s32[1,256]{1,0:T(1,128)} %bitcast.21), custom_call_target="tpu_custom_call" | custom-call | flops 10000000 | bytes 100000 | tf_op jit(solution)/shard_map/prep/pallas_call | solution.py:281
  2.5 14.4 %all_to_all.31 = s32[32,1,24]{2,1,0:T(1,128)S(1)} all-to-all(s32[32,1,24]{2,1,0:T(1,128)} %bitcast.19), channel_id=1, replica_groups=mesh['gx'=8,'gz'=4] {'gx','gz'}, dimensions={0} | all-to-all | bytes 6144 | tf_op jit(solution)/shard_map/all_to_all | solution.py:289
  16.9 0.5 broadcast.3
  17.4 0.7 reduce.3
  18.1 0.7 reshape.31.index_ref
  18.8 6.2 %gather.1 = bf16[768,384]{1,0:T(8,128)(2,1)} custom-call(s32[1,768]{1,0:T(1,128)} %reshape.31.index_ref, f32[3,6144,128]{2,1,0:T(8,128)} %bitcast.12), custom_call_target="tpu_custom_call" | custom-call | flops 1000000 | bytes 9437184 | tf_op jit(solution)/shard_map/gather/pallas_call | solution.py:312
  25.0 2.6 %all-to-all-start.1 = ((bf16[32,24,384]{2,1,0:T(8,128)(2,1)}), bf16[32,24,384]{2,1,0:T(8,128)(2,1)S(1)}, u32[]{:S(2)}, u32[]{:S(2)}) async-start(bf16[32,24,384]{2,1,0:T(8,128)(2,1)} %bitcast.17), calls=%async_computation.1 | async-start | bytes 1179648 | tf_op jit(solution)/shard_map/all_to_all | solution.py:322
  28.3 16.1 %all-to-all-done.1 = bf16[32,24,384]{2,1,0:T(8,128)(2,1)S(1)} async-done(((bf16[32,24,384]{2,1,0:T(8,128)(2,1)}), bf16[32,24,384]{2,1,0:T(8,128)(2,1)S(1)}, u32[]{:S(2)}, u32[]{:S(2)}) %all-to-all-start.1) | async-done | bytes 589856 | tf_op jit(solution)/shard_map/all_to_all | solution.py:322
  44.4 0.0 copy-start.1
  44.4 0.8 copy-done.1
  45.2 10.7 %particles.1 = (f32[3,64,128]{2,1,0:T(8,128)}, bf16[768,384]{1,0:T(8,128)(2,1)}) custom-call(s32[1]{0:T(128)S(6)} %copy.9.live_ref, s32[256,1]{1,0:T(8,128)} %get-tuple-element.15.slot_ref, bf16[768,384]{1,0:T(8,128)(2,1)} %bitcast.16, bf16[64,128,512]{2,1,0:T(8,128)(2,1)} %weight_ref.1, f32[3,64,128]{2,1,0:T(8,128)} %velocity_ref.1), custom_call_target="tpu_custom_call" | custom-call | flops 400000000 | bytes 8388608 | tf_op jit(solution)/shard_map/particles/pallas_call | solution.py:351
  55.9 3.2 %all-to-all-start.2 = ((bf16[32,24,384]{2,1,0:T(8,128)(2,1)}), bf16[32,24,384]{2,1,0:T(8,128)(2,1)S(1)}, u32[]{:S(2)}, u32[]{:S(2)}) async-start(bf16[32,24,384]{2,1,0:T(8,128)(2,1)} %bitcast.18), calls=%async_computation.2 | async-start | bytes 1179648 | tf_op jit(solution)/shard_map/all_to_all | solution.py:374
  59.1 6.7 %edges.1 = (f32[9,16,128]{2,1,0:T(8,128)}, f32[9,16,128]{2,1,0:T(8,128)}, bf16[3,1,6144]{2,1,0:T(2,128)(2,1)}, bf16[3,1,6144]{2,1,0:T(2,128)(2,1)}) custom-call(f32[3,384,16,128]{3,2,1,0:T(8,128)} %u_ref.3), custom_call_target="tpu_custom_call" | custom-call | flops 10000000 | bytes 9437184 | tf_op jit(solution)/shard_map/edges/pallas_call | solution.py:294
  65.8 1.8 %collective-permute-start.2 = (f32[9,16,128]{2,1,0:T(8,128)}, f32[9,16,128]{2,1,0:T(8,128)S(1)}, u32[]{:S(2)}, u32[]{:S(2)}) collective-permute-start(f32[9,16,128]{2,1,0:T(8,128)} %get-tuple-element.13), channel_id=1, source_target_pairs={{0,4},{4,8},{8,12},{12,16},{16,20},{20,24},{24,28},{28,0},{1,5},{5... | collective-permute-start | bytes 221192 | tf_op jit(solution)/shard_map/ppermute | solution.py:307
  67.6 3.0 %collective-permute-start.3 = (f32[9,16,128]{2,1,0:T(8,128)}, f32[9,16,128]{2,1,0:T(8,128)S(1)}, u32[]{:S(2)}, u32[]{:S(2)}) collective-permute-start(f32[9,16,128]{2,1,0:T(8,128)} %get-tuple-element.14), channel_id=1, source_target_pairs={{4,0},{8,4},{12,8},{16,12},{20,16},{24,20},{28,24},{0,28},{5,1},{9... | collective-permute-start | bytes 221192 | tf_op jit(solution)/shard_map/ppermute | solution.py:308
  70.5 0.0 collective-permute-start
  70.5 1.7 %collective-permute-start.1 = (bf16[3,1,6144]{2,1,0:T(2,128)(2,1)}, bf16[3,1,6144]{2,1,0:T(2,128)(2,1)S(1)}, u32[]{:S(2)}, u32[]{:S(2)}) collective-permute-start(bf16[3,1,6144]{2,1,0:T(2,128)(2,1)} %get-tuple-element.12), channel_id=1, source_target_pairs={{1,0},{2,1},{3,2},{0,3},{5,4},{6,5},{7,6},{4,7},{9,8},{10,9},{11,1... | collective-permute-start | bytes 110600 | tf_op jit(solution)/shard_map/ppermute | solution.py:310
  72.3 2.7 %collective-permute-done.low_ref = bf16[3,1,6144]{2,1,0:T(2,128)(2,1)S(1)} collective-permute-done((bf16[3,1,6144]{2,1,0:T(2,128)(2,1)}, bf16[3,1,6144]{2,1,0:T(2,128)(2,1)S(1)}, u32[]{:S(2)}, u32[]{:S(2)}) %collective-permute-start) | collective-permute-done | bytes 36896 | tf_op jit(solution)/shard_map/ppermute | solution.py:309
  75.0 0.0 copy-start.4
  75.0 0.1 collective-permute-done.1.high_ref
  75.1 0.0 copy-start.5
  75.1 0.9 collective-permute-done.2.left_ref
  76.0 0.0 copy-start.2
  76.0 0.0 collective-permute-done.3.right_ref
  76.0 0.0 copy-done.4
  76.0 0.0 copy-done.5
  76.0 0.6 copy-done.2
  76.6 0.0 copy-start.3
  76.6 0.6 copy-done.3
  77.2 28.0 %deriv.1 = f32[3,384,16,128]{3,2,1,0:T(8,128)} custom-call(f32[3,384,16,128]{3,2,1,0:T(8,128)} %u_ref.3, bf16[3,1,6144]{2,1,0:T(2,128)(2,1)} %copy-done.4, bf16[3,1,6144]{2,1,0:T(2,128)(2,1)} %copy-done.5, f32[9,16,128]{2,1,0:T(8,128)} %copy-done.2, f32[9,16,128]{2,1,0:T(8,128)} %copy-done.3), custom_call_target="tpu_custom_call" | custom-call | flops 94371840 | bytes 28311552 | tf_op jit(solution)/shard_map/deriv/pallas_call | solution.py:326
  105.3 0.0 all-to-all-done.2
  105.3 0.0 copy-start
  105.3 0.8 copy-done
  106.1 13.7 %feedback.1 = f32[3,6144,128]{2,1,0:T(8,128)} custom-call(s32[1,768]{1,0:T(1,128)} %reshape.31.index_ref, f32[3,6144,128]{2,1,0:T(8,128)} %bitcast.13, bf16[768,384]{1,0:T(8,128)(2,1)} %bitcast.15), custom_call_target="tpu_custom_call" | custom-call | flops 3623878656 | bytes 18874368 | tf_op jit(solution)/shard_map/feedback/pallas_call | solution.py:377
Async XLA Ops:
  25.0 19.3 %all-to-all-start.1 = ((bf16[32,24,384]{2,1,0:T(8,128)(2,1)}), bf16[32,24,384]{2,1,0:T(8,128)(2,1)S(1)}, u32[]{:S(2)}, u32[]{:S(2)}) async-start(bf16[32,24,384]{2,1,0:T(8,128)(2,1)} %bitcast.17), calls=%async_computation.1 | async-start | bytes 1179648 | tf_op jit(solution)/shard_map/all_to_all | solution.py:322
  44.4 0.8 copy-start.1
  55.9 49.4 %all-to-all-start.2 = ((bf16[32,24,384]{2,1,0:T(8,128)(2,1)}), bf16[32,24,384]{2,1,0:T(8,128)(2,1)S(1)}, u32[]{:S(2)}, u32[]{:S(2)}) async-start(bf16[32,24,384]{2,1,0:T(8,128)(2,1)} %bitcast.18), calls=%async_computation.2 | async-start | bytes 1179648 | tf_op jit(solution)/shard_map/all_to_all | solution.py:374
  65.8 10.2 %collective-permute-start.2 = (f32[9,16,128]{2,1,0:T(8,128)}, f32[9,16,128]{2,1,0:T(8,128)S(1)}, u32[]{:S(2)}, u32[]{:S(2)}) collective-permute-start(f32[9,16,128]{2,1,0:T(8,128)} %get-tuple-element.13), channel_id=1, source_target_pairs={{0,4},{4,8},{8,12},{12,16},{16,20},{20,24},{24,28},{28,0},{1,5},{5... | collective-permute-start | bytes 221192 | tf_op jit(solution)/shard_map/ppermute | solution.py:307
  67.6 8.4 %collective-permute-start.3 = (f32[9,16,128]{2,1,0:T(8,128)}, f32[9,16,128]{2,1,0:T(8,128)S(1)}, u32[]{:S(2)}, u32[]{:S(2)}) collective-permute-start(f32[9,16,128]{2,1,0:T(8,128)} %get-tuple-element.14), channel_id=1, source_target_pairs={{4,0},{8,4},{12,8},{16,12},{20,16},{24,20},{28,24},{0,28},{5,1},{9... | collective-permute-start | bytes 221192 | tf_op jit(solution)/shard_map/ppermute | solution.py:308
  70.5 4.4 %collective-permute-start = (bf16[3,1,6144]{2,1,0:T(2,128)(2,1)}, bf16[3,1,6144]{2,1,0:T(2,128)(2,1)S(1)}, u32[]{:S(2)}, u32[]{:S(2)}) collective-permute-start(bf16[3,1,6144]{2,1,0:T(2,128)(2,1)} %get-tuple-element.11), channel_id=1, source_target_pairs={{0,1},{1,2},{2,3},{3,0},{4,5},{5,6},{6,7},{7,4},{8,9},{9,10},{10,1... | collective-permute-start | bytes 110600 | tf_op jit(solution)/shard_map/ppermute | solution.py:309
  70.5 4.5 %collective-permute-start.1 = (bf16[3,1,6144]{2,1,0:T(2,128)(2,1)}, bf16[3,1,6144]{2,1,0:T(2,128)(2,1)S(1)}, u32[]{:S(2)}, u32[]{:S(2)}) collective-permute-start(bf16[3,1,6144]{2,1,0:T(2,128)(2,1)} %get-tuple-element.12), channel_id=1, source_target_pairs={{1,0},{2,1},{3,2},{0,3},{5,4},{6,5},{7,6},{4,7},{9,8},{10,9},{11,1... | collective-permute-start | bytes 110600 | tf_op jit(solution)/shard_map/ppermute | solution.py:310
  75.0 1.1 copy-start.4
  75.1 0.9 copy-start.5
  76.0 0.6 copy-start.2
  76.6 0.6 copy-start.3
  105.3 0.8 copy-start
where the time goes:
time: 121 us; the launch traced here: 120 us
  Pallas kernels  67.2 us (56%)
  waiting for transfers between devices  19.8 us (16%)
  blocking collectives  14.4 us (12%)
  starting transfers between devices  12.3 us (10%)
  local copies, waits for them, and re-layouts  4.06 us (3%)
  between operations  1.33 us (1%)
    pallas_call x1, Pallas kernels, shards(): pl.pallas_call(deriv_kernel, grid=(2 * parts,), out_shape=shape(velocity_...  28 us
    all_to_all x1, waiting for transfers between devices, shards(): lax.all_to_all(tile_data, ('gx', 'gz'), split_axis=0, concat_axis=0, tile...  16.1 us
    all_to_all x1, blocking collectives, shards(): lax.all_to_all(send_index, ('gx', 'gz'), split_axis=0, concat_axis=0, til...  14.4 us
    pallas_call x1, Pallas kernels, shards(): pl.pallas_call(add_kernel, grid=(lines // chunk,), out_shape=shape((3, li...  13.7 us
    pallas_call x1, Pallas kernels, shards(): pl.pallas_call(functools.partial(particle_kernel, kt), grid=(blocks // gr...  10.7 us
    pallas_call x1, Pallas kernels, shards(): pl.pallas_call(edge_kernel, grid=(slab // window,), out_shape=(shape((9,...  6.67 us
    pallas_call x1, Pallas kernels, shards(): pl.pallas_call(gather_kernel, out_shape=shape((slots, 3 * span), BF16), i...  6.25 us
    all_to_all x1, starting transfers between devices, shards(): lax.all_to_all(outgoing, ('gx', 'gz'), split_axis=0, concat_axis=0, tiled...  3.2 us
  transfers between devices with their start and end apart: 6, of which 4 were waited for; matrix products, arithmetic and copies ran while one was open for 0% of the time, Pallas kernels for 29%

commit v1 on v0

v1 whole, which is shorter than its diff:
```python
import functools
import math

import jax
import jax.numpy as jnp
from jax import lax
from jax.experimental import pallas as pl
from jax.experimental.pallas import tpu as pltpu
from jax.sharding import PartitionSpec as P

ROOT = (math.sqrt(5.0) / 3.0 - 1.0) * 1.5
GREEN_GAIN = 3.0 / math.sqrt(5.0)
GAMMA = (25.0 / 36.0) * GREEN_GAIN * (1.0 - ROOT * ROOT)
EPS = (1.0 / 12.0) / GAMMA
VISCOSITY = 0.2
RELAX_TIME = 1.0
TIME_STEP = 0.5
LOADING = 0.5
WINDOW = 96
F32 = jnp.float32
BF16 = jnp.bfloat16
VMEM_LIMIT = 56 * 1024 * 1024


def iota(shape, dim):
    return lax.broadcasted_iota(jnp.int32, shape, dim)


def dot(a, b, ca, cb):
    return lax.dot_general(a, b, (((ca,), (cb,)), ((), ())), preferred_element_type=F32)


def end_lanes(span):
    corner = (8, span)
    first = (iota(corner, 0) == 0) & (iota(corner, 1) == 0)
    second = (iota(corner, 0) == 1) & (iota(corner, 1) == span - 1)
    return jnp.where(first | second, 1.0, 0.0)


def request_slots(kt, capacity, devices, owner_row, index_row):
    count = owner_row.shape[1]
    blocks = count // kt
    rows, cols = iota((count, count), 0), iota((count, count), 1)
    pick = cols == kt * (rows % blocks) + rows // blocks
    owner = jnp.sum(jnp.where(pick, owner_row, 0), 1, keepdims=True)
    index = jnp.sum(jnp.where(pick, index_row, 0), 1, keepdims=True)
    onehot = (owner == iota((count, devices), 1)).astype(F32)
    lower = (cols <= rows).astype(F32).astype(BF16)
    seen = dot(lower, onehot.astype(BF16), 1, 0)
    position = jnp.sum(seen * onehot, 1, keepdims=True).astype(jnp.int32) - 1
    place = position == iota((count, 128), 1)
    high = jnp.where(place, (index // 128).astype(F32), 0.0).astype(BF16)
    low = jnp.where(place, (index % 128).astype(F32), 0.0).astype(BF16)
    turned = onehot.astype(BF16)
    high_sum, low_sum = dot(turned, high, 0, 0), dot(turned, low, 0, 0)
    send = high_sum.astype(jnp.int32) * 128 + low_sum.astype(jnp.int32)
    return owner * capacity + position, send


def row_fields(ref, i):
    u = [ref[c, i] for c in range(3)]
    return u + [u[0] * u[c] for c in range(3)]


def exchange_kernel(
    sizes, owner_ref, index_ref, field_hbm,
    tile_ref, slot_ref, got_ref, low_ref, high_ref, left_ref, right_ref,
    field_ref, table_ref, send_ref, got_smem, rows_ref, my_low, my_high, my_left, my_right,
    field_sem, smem_sem, send_sem, recv_sem, edge_send, edge_recv,
):
    gx, gz, kt, capacity, window = sizes
    devices = gx * gz
    wall, span = my_left.shape[1:]
    lines = field_ref.shape[1]
    slab = lines // wall
    x, z = lax.axis_index("gx"), lax.axis_index("gz")
    me = x * gz + z
    fetch = pltpu.make_async_copy(field_hbm, field_ref, field_sem)
    fetch.start()

    barrier = pltpu.get_barrier_semaphore()

    def greet(d, carry):
        peer = lax.rem(me + d, devices)
        pl.semaphore_signal(
            barrier, inc=1, device_id=(peer // gz, lax.rem(peer, gz)), device_id_type=pl.DeviceIdType.MESH
        )
        return carry

    lax.fori_loop(1, devices, greet, 0)
    slot, send = request_slots(kt, capacity, devices, owner_ref[...], index_ref[...])
    slot_ref[...] = slot
    table_ref[...] = send
    for d in range(devices):
        send_ref[d] = table_ref[d : d + 1, :]
    pl.semaphore_wait(barrier, devices - 1)

    def parcel(d):
        peer = lax.rem(me + d, devices)
        return pltpu.make_async_remote_copy(
            src_ref=send_ref.at[peer],
            dst_ref=got_ref.at[me],
            send_sem=send_sem.at[d],
            recv_sem=recv_sem.at[d],
            device_id=(peer // gz, lax.rem(peer, gz)),
            device_id_type=pl.DeviceIdType.MESH,
        )

    def post(d, carry):
        parcel(d).start()
        return carry

    lax.fori_loop(1, devices, post, 0)
    got_ref[me] = send_ref[me]
    fetch.wait()

    def edge(k, src, dst, peer):
        return pltpu.make_async_remote_copy(
            src_ref=src,
            dst_ref=dst,
            send_sem=edge_send.at[k],
            recv_sem=edge_recv.at[k],
            device_id=peer,
            device_id_type=pl.DeviceIdType.MESH,
        )

    edges = [
        edge(0, my_right, left_ref, (lax.rem(x + 1, gx), z)),
        edge(1, my_left, right_ref, (lax.rem(x + gx - 1, gx), z)),
        edge(2, my_high, low_ref, (x, lax.rem(z + 1, gz))),
        edge(3, my_low, high_ref, (x, lax.rem(z + gz - 1, gz))),
    ]

    def moments(order):
        def one(i, state):
            at = pl.ds(pl.multiple_of(order(i) * wall, wall), wall)
            u = [field_ref[c, at, :] for c in range(3)]
            fields = u + [u[0] * u[c] for c in range(3)]
            return tuple(f + ROOT * s for f, s in zip(fields, state))

        return lax.fori_loop(0, window, one, (jnp.zeros((wall, span), F32),) * 6, unroll=4)

    for k, value in enumerate(moments(lambda i: slab - window + i)):
        my_right[k] = value
    for c in range(3):
        my_right[6 + c] = field_ref[c, lines - wall :, :]
    edges[0].start()
    for k, value in enumerate(moments(lambda i: window - 1 - i)):
        my_left[k] = value
    for c in range(3):
        my_left[6 + c] = field_ref[c, :wall, :]
    edges[1].start()

    def arrive(d, carry):
        parcel(d).wait()
        return carry

    lax.fori_loop(1, devices, arrive, 0)
    copy = pltpu.make_async_copy(got_ref, got_smem, smem_sem)
    copy.start()
    copy.wait()

    def gather(d, carry):
        for k in range(capacity):
            row = jnp.minimum(jnp.maximum(got_smem[d, 0, k], 0), lines - 1)
            for c in range(3):
                rows_ref[c, pl.ds(d * capacity + k, 1), :] = field_ref[c, pl.ds(row, 1), :]
        return carry

    lax.fori_loop(0, devices, gather, 0)
    for c in range(3):
        tile_ref[:, c * span : (c + 1) * span] = rows_ref[c].astype(BF16)

    pick = end_lanes(span).astype(BF16)
    for c in range(3):
        for n in range(slab // window):
            part = slice(n * window * wall, (n + 1) * window * wall)
            lanes = dot(pick, field_ref[c, part].astype(BF16), 1, 1)
            my_low[c, :, part] = lanes[0:1]
            my_high[c, :, part] = lanes[1:2]
    edges[2].start()
    edges[3].start()
    for copy in edges:
        copy.wait()


def load_state(state_ref, edge_ref):
    edge = [edge_ref[6 + c] for c in range(3)]
    edge = edge + [edge[0] * edge[c] for c in range(3)]
    for k in range(6):
        state_ref[k] = edge_ref[k]
        state_ref[6 + k] = edge[k]


def advance(u_ref, i, carry):
    state, before = carry[:6], carry[6:]
    fields = row_fields(u_ref, i)
    parts = [EPS * f + s for f, s in zip(before, state)]
    sums = [parts[3 + c] + fields[0] * parts[c] for c in range(3)]
    moved = [f + ROOT * s for f, s in zip(fields, state)]
    return fields, sums, tuple(moved) + tuple(fields)


def up_kernel(u_ref, low_ref, high_ref, left_ref, out_ref, state_ref, halo_ref):
    rows, wall, span = u_ref.shape[1:]
    lane = iota((wall, span), 1)

    @pl.when(pl.program_id(0) == 0)
    def _():
        load_state(state_ref, left_ref)

    shape = (8, rows * wall)
    pick = end_lanes(span)
    for c in range(3):
        ends = jnp.where(iota(shape, 0) == 0, low_ref[c], jnp.where(iota(shape, 0) == 1, high_ref[c], 0.0))
        halo_ref[c] = dot(ends, pick, 0, 0).reshape(rows, wall, span)

    def one(i, carry):
        fields, sums, carry = advance(u_ref, i, carry)
        for c in range(3):
            u = fields[c]
            near = jnp.where(lane == 0, 0.0, pltpu.roll(u, 1, 1))
            far = jnp.where(lane == span - 1, 0.0, pltpu.roll(u, span - 1, 1))
            curve = near + far + halo_ref[c, i] - 2.0 * u
            out_ref[c, i] = 0.5 * GAMMA * sums[c] + VISCOSITY * curve
        return carry

    end = lax.fori_loop(0, rows, one, tuple(state_ref[k] for k in range(12)), unroll=4)
    for k in range(12):
        state_ref[k] = end[k]


def down_kernel(u_ref, part_ref, right_ref, out_ref, state_ref):
    rows = u_ref.shape[1]

    @pl.when(pl.program_id(0) == 0)
    def _():
        load_state(state_ref, right_ref)

    def one(n, carry):
        i = rows - 1 - n
        _, sums, carry = advance(u_ref, i, carry)
        for c in range(3):
            out_ref[c, i] = part_ref[c, i] - 0.5 * GAMMA * sums[c]
        return carry

    end = lax.fori_loop(0, rows, one, tuple(state_ref[k] for k in range(12)), unroll=4)
    for k in range(12):
        state_ref[k] = end[k]


def particle_kernel(kt, live_ref, slot_ref, reply_ref, weight_ref, velocity_ref, moved_ref, out_ref, own_ref, push_ref):
    step, last = pl.program_id(0), pl.num_programs(0) - 1
    group, particles, cells = weight_ref.shape
    count, slots = slot_ref.shape[0], reply_ref.shape[0]
    span = cells // kt
    blocks = count // kt

    @pl.when(step == 0)
    def _():
        chosen = jnp.where(slot_ref[...] == iota((count, slots), 1), 1.0, 0.0).astype(BF16)
        own = dot(chosen, reply_ref[...], 1, 0)
        for j in range(kt):
            for c in range(3):
                own_ref[c, :, j * span : (j + 1) * span] = own[
                    j * blocks : (j + 1) * blocks, c * span : (c + 1) * span
                ]

    base = pl.multiple_of(step * group, group)
    tiles = jnp.concatenate([own_ref[c, pl.ds(base, group), :] for c in range(3)], 0).astype(BF16)
    row = iota((3 * group, particles), 0) % group
    sampled = jnp.zeros((3 * group, particles), F32)
    for b in range(group):
        sampled = jnp.where(row == b, dot(tiles, weight_ref[b], 1, 1), sampled)
    velocity = velocity_ref[...].reshape(3 * group, particles)
    live = jnp.where(row + base < live_ref[0], 1.0, 0.0)
    drag = live * (sampled - velocity) * (1.0 / RELAX_TIME)
    moved_ref[...] = (velocity + TIME_STEP * drag).reshape(3, group, particles)
    half = drag.astype(BF16)
    row = iota((3 * group, cells), 0) % group
    push = jnp.zeros((3 * group, cells), F32)
    for b in range(group):
        push = jnp.where(row == b, dot(half, weight_ref[b], 1, 0), push)
    push = -LOADING * push
    for j in range(kt):
        for c in range(3):
            push_ref[pl.ds(j * blocks + base, group), c * span : (c + 1) * span] = push[
                c * group : (c + 1) * group, j * span : (j + 1) * span
            ]

    @pl.when(step == last)
    def _():
        same = iota((count, count), 0) == iota((count, count), 1)
        slot_row = jnp.sum(jnp.where(same, slot_ref[...], 0), 0, keepdims=True)
        placed = jnp.where(iota((slots, count), 0) == slot_row, 1.0, 0.0).astype(BF16)
        out_ref[...] = dot(placed, push_ref[...].astype(BF16), 1, 0).astype(BF16)


def add_kernel(index_ref, base_ref, back_ref, out_ref):
    rows, span = base_ref.shape[1:]
    slots = back_ref.shape[0]
    for n in range(rows // 256):
        local = index_ref[...] - (pl.program_id(0) * rows + n * 256)
        local = jnp.where((local >= 0) & (local < 256), local, -1).astype(F32).astype(BF16)
        ids = iota((256, slots), 0).astype(F32).astype(BF16)
        named = jnp.where(ids == local, jnp.ones((), BF16), jnp.zeros((), BF16))
        total = dot(named, back_ref[...], 1, 0)
        part = slice(n * 256, (n + 1) * 256)
        for c in range(3):
            out_ref[c, part] = base_ref[c, part] + total[:, c * span : (c + 1) * span]


def vmem():
    return pl.BlockSpec(memory_space=pltpu.VMEM)


def smem():
    return pl.BlockSpec(memory_space=pltpu.SMEM)


def params():
    return pltpu.CompilerParams(vmem_limit_bytes=VMEM_LIMIT)


def cost(flops, nbytes):
    return pl.CostEstimate(flops=int(flops), bytes_accessed=int(nbytes), transcendentals=0)


def largest_divisor(total, limit):
    return max(d for d in range(1, limit + 1) if total % d == 0)


def shards(velocity_field, interp_weight, particle_velocity, tile_owner, tile_index, block_count):
    _, slab, wall, span = velocity_field.shape
    shape = jax.ShapeDtypeStruct
    gx, gz = lax.axis_size("gx"), lax.axis_size("gz")
    devices = gx * gz
    requests = tile_index.shape[0]
    blocks, particles, cells = interp_weight.shape
    kt = requests // blocks
    capacity = max(2, 3 * requests // devices)
    slots = devices * capacity
    field_bytes = velocity_field.size * 4

    window = WINDOW if slab % WINDOW == 0 else slab
    lines = slab * wall
    dma = pltpu.SemaphoreType.DMA
    tile_data, slot_ids, got, from_low, from_high, from_left, from_right = pl.pallas_call(
        functools.partial(exchange_kernel, (gx, gz, kt, capacity, window)),
        out_shape=(
            shape((slots, 3 * span), BF16),
            shape((requests, 1), jnp.int32),
            shape((devices, 1, 128), jnp.int32),
            shape((3, 1, lines), F32),
            shape((3, 1, lines), F32),
            shape((9, wall, span), F32),
            shape((9, wall, span), F32),
        ),
        in_specs=[vmem(), vmem(), pl.BlockSpec(memory_space=pl.ANY)],
        out_specs=(vmem(),) * 7,
        scratch_shapes=[
            pltpu.VMEM((3, lines, span), F32),
            pltpu.VMEM((devices, 128), jnp.int32),
            pltpu.VMEM((devices, 1, 128), jnp.int32),
            pltpu.SMEM((devices, 1, 128), jnp.int32),
            pltpu.VMEM((3, slots, span), F32),
            pltpu.VMEM((3, 1, lines), F32),
            pltpu.VMEM((3, 1, lines), F32),
            pltpu.VMEM((9, wall, span), F32),
            pltpu.VMEM((9, wall, span), F32),
            dma,
            dma,
            dma((devices,)),
            dma((devices,)),
            dma((4,)),
            dma((4,)),
        ],
        compiler_params=pltpu.CompilerParams(
            vmem_limit_bytes=VMEM_LIMIT, collective_id=0, has_side_effects=True
        ),
        cost_estimate=cost(1e7, field_bytes),
        name="exchange",
    )(tile_owner.reshape(1, requests), tile_index.reshape(1, requests), velocity_field.reshape(3, lines, span))
    got = got[:, 0, :capacity].reshape(1, slots)
    replies = lax.all_to_all(tile_data, ("gx", "gz"), split_axis=0, concat_axis=0, tiled=True)

    rows = largest_divisor(slab, 48)
    parts = slab // rows
    up_part = pl.pallas_call(
        up_kernel,
        grid=(parts,),
        out_shape=shape(velocity_field.shape, F32),
        in_specs=[
            pl.BlockSpec((3, rows, wall, span), lambda i: (0, i, 0, 0)),
            pl.BlockSpec((3, 1, rows * wall), lambda i: (0, 0, i)),
            pl.BlockSpec((3, 1, rows * wall), lambda i: (0, 0, i)),
            pl.BlockSpec((9, wall, span), lambda i: (0, 0, 0)),
        ],
        out_specs=pl.BlockSpec((3, rows, wall, span), lambda i: (0, i, 0, 0)),
        scratch_shapes=[pltpu.VMEM((12, wall, span), F32), pltpu.VMEM((3, rows, wall, span), F32)],
        compiler_params=params(),
        cost_estimate=cost(velocity_field.size * 20, field_bytes * 2),
        name="up",
    )(velocity_field, from_low, from_high, from_left)
    replies, up_part = lax.optimization_barrier((replies, up_part))

    group = 8
    moved, outgoing = pl.pallas_call(
        functools.partial(particle_kernel, kt),
        grid=(blocks // group,),
        out_shape=(shape(particle_velocity.shape, F32), shape((slots, 3 * span), BF16)),
        in_specs=[
            smem(),
            pl.BlockSpec((requests, 1), lambda i: (0, 0)),
            pl.BlockSpec((slots, 3 * span), lambda i: (0, 0)),
            pl.BlockSpec((group, particles, cells), lambda i: (i, 0, 0)),
            pl.BlockSpec((3, group, particles), lambda i: (0, i, 0)),
        ],
        out_specs=(
            pl.BlockSpec((3, group, particles), lambda i: (0, i, 0)),
            pl.BlockSpec((slots, 3 * span), lambda i: (0, 0)),
        ),
        scratch_shapes=[
            pltpu.VMEM((3, blocks, cells), F32),
            pltpu.VMEM((requests, 3 * span), F32),
        ],
        compiler_params=params(),
        cost_estimate=cost(4e8, interp_weight.size * 2),
        name="particles",
    )(block_count, slot_ids, replies, interp_weight, particle_velocity)
    outgoing, up_part = lax.optimization_barrier((outgoing, up_part))
    returned = lax.all_to_all(outgoing, ("gx", "gz"), split_axis=0, concat_axis=0, tiled=True)
    fluid = pl.pallas_call(
        down_kernel,
        grid=(parts,),
        out_shape=shape(velocity_field.shape, F32),
        in_specs=[
            pl.BlockSpec((3, rows, wall, span), lambda i: (0, parts - 1 - i, 0, 0)),
            pl.BlockSpec((3, rows, wall, span), lambda i: (0, parts - 1 - i, 0, 0)),
            pl.BlockSpec((9, wall, span), lambda i: (0, 0, 0)),
        ],
        out_specs=pl.BlockSpec((3, rows, wall, span), lambda i: (0, parts - 1 - i, 0, 0)),
        scratch_shapes=[pltpu.VMEM((12, wall, span), F32)],
        compiler_params=params(),
        cost_estimate=cost(velocity_field.size * 20, field_bytes * 3),
        name="down",
    )(velocity_field, up_part, from_right)

    chunk = 512 if lines % 512 == 0 else lines
    result = pl.pallas_call(
        add_kernel,
        grid=(lines // chunk,),
        out_shape=shape((3, lines, span), F32),
        in_specs=[
            pl.BlockSpec((1, slots), lambda i: (0, 0)),
            pl.BlockSpec((3, chunk, span), lambda i: (0, i, 0)),
            pl.BlockSpec((slots, 3 * span), lambda i: (0, 0)),
        ],
        out_specs=pl.BlockSpec((3, chunk, span), lambda i: (0, i, 0)),
        compiler_params=params(),
        cost_estimate=cost(2.0 * lines * slots * 3 * span, field_bytes * 2),
        name="feedback",
    )(got, fluid.reshape(3, lines, span), returned)
    return (result.reshape(velocity_field.shape), moved)


def solution(mesh):
    placed = (
        P(None, "gx", None, "gz"),
        P(("gx", "gz"), None, None),
        P(None, ("gx", "gz"), None),
        P(("gx", "gz"), None),
        P(("gx", "gz")),
        P(("gx", "gz")),
    )
    return jax.shard_map(
        shards,
        mesh=mesh,
        in_specs=placed,
        out_specs=(P(None, "gx", None, "gz"), P(None, ("gx", "gz"), None)),
        check_vma=False,
    )
```

time: 121 us -> 92.4 us (0.76)
  waiting for transfers between devices: 19.8 us -> 2.58 us
  blocking collectives: 14.4 us -> 0 us
  Pallas kernels: 67.2 us -> 74.8 us
  starting transfers between devices: 12.3 us -> 10.4 us
  local copies, waits for them, and re-layouts: 4.06 us -> 2.36 us
    all_to_all x1, waiting for transfers between devices: 16.1 us -> 0.01 us  [shards(): lax.all_to_all(tile_data, ('gx', 'gz'), split_axis=0, concat_axis=0, tile...]
    all_to_all x1 -> x0, blocking collectives: 14.4 us -> none  [shards(): lax.all_to_all(send_index, ('gx', 'gz'), split_axis=0, concat_axis=0, til...]
    pallas_call x4 -> x3, Pallas kernels: 42.8 us -> 50.5 us  [the longest x1 18.6 us: shards(): pl.pallas_call(functools.partial(exchange_kernel, (gx, gz, kt, capacity,...]
    ppermute x4 -> x0, starting transfers between devices: 6.52 us -> none  [the longest x1 2.95 us: shards(): from_right = lax.ppermute(to_left, 'gx', behind(gx))]
    ppermute x4 -> x0, waiting for transfers between devices: 3.71 us -> none  [the longest x1 2.66 us: shards(): from_low = lax.ppermute(high, 'gz', ahead(gz))]
    all_to_all x1, starting transfers between devices: 3.2 us -> 5.83 us  [shards(): lax.all_to_all(outgoing, ('gx', 'gz'), split_axis=0, concat_axis=0, tiled...]
    all_to_all x1, waiting for transfers between devices: 0.01 us -> 2.58 us  [shards(): lax.all_to_all(outgoing, ('gx', 'gz'), split_axis=0, concat_axis=0, tiled...]
    all_to_all x1, starting transfers between devices: 2.61 us -> 4.61 us  [shards(): lax.all_to_all(tile_data, ('gx', 'gz'), split_axis=0, concat_axis=0, tile...]
  transfers between devices with their start and end apart: 6 -> 2, of which waited for: 4 -> 1; matrix products, arithmetic and copies ran while one was open for 0% -> 1% of each run, Pallas kernels for 29% -> 35%
where the time goes in v1:
time: 92.4 us; the launch traced here: 91.5 us
  Pallas kernels  74.8 us (81%)
  starting transfers between devices  10.4 us (11%)
  waiting for transfers between devices  2.58 us (3%)
  local copies, waits for them, and re-layouts  2.36 us (3%)
  between operations  1.33 us (1%)
    pallas_call x1, Pallas kernels, shards(): pl.pallas_call(functools.partial(exchange_kernel, (gx, gz, kt, capacity,...  18.6 us
    pallas_call x1, Pallas kernels, shards(): pl.pallas_call(up_kernel, grid=(parts,), out_shape=shape(velocity_field.s...  18.5 us
    pallas_call x1, Pallas kernels, shards(): pl.pallas_call(add_kernel, grid=(lines // chunk,), out_shape=shape((3, li...  13.6 us
    pallas_call x1, Pallas kernels, shards(): pl.pallas_call(down_kernel, grid=(parts,), out_shape=shape(velocity_field...  13.4 us
    pallas_call x1, Pallas kernels, shards(): pl.pallas_call(functools.partial(particle_kernel, kt), grid=(blocks // gr...  10.7 us
    all_to_all x1, starting transfers between devices, shards(): lax.all_to_all(outgoing, ('gx', 'gz'), split_axis=0, concat_axis=0, tiled...  5.83 us
    all_to_all x1, starting transfers between devices, shards(): lax.all_to_all(tile_data, ('gx', 'gz'), split_axis=0, concat_axis=0, tile...  4.61 us
    all_to_all x1, waiting for transfers between devices, shards(): lax.all_to_all(outgoing, ('gx', 'gz'), split_axis=0, concat_axis=0, tiled...  2.58 us
  transfers between devices with their start and end apart: 2, of which 1 were waited for; matrix products, arithmetic and copies ran while one was open for 1% of the time, Pallas kernels for 35%

profile of v1, /device:TPU:0, one launch (start us, length us, event | category | flops | bytes accessed | tf_op | source)
XLA Modules:
  0.0 91.5 jit_solution(12461017463526284236)
XLA Ops:
  0.6 18.6 %exchange.1 = (bf16[768,384]{1,0:T(8,128)(2,1)}, s32[256,1]{1,0:T(8,128)}, s32[32,1,128]{2,1,0:T(1,128)}, f32[3,1,6144]{2,1,0:T(1,128)}, f32[3,1,6144]{2,1,0:T(1...) custom-call(s32[1,256]{1,0:T(1,128)} %bitcast.16, s32[1,256]{1,0:T(1,128)} %bitcast.17, f32[3,6144,128]{2,1,0:T(8,128)} %bitcast.9), custom_call_target="tpu_custom_call" | custom-call | flops 10000000 | bytes 9437184 | tf_op jit(solution)/shard_map/exchange/pallas_call | solution.py:348
  19.2 4.6 %all-to-all-start = ((bf16[32,24,384]{2,1,0:T(8,128)(2,1)}), bf16[32,24,384]{2,1,0:T(8,128)(2,1)S(1)}, u32[]{:S(2)}, u32[]{:S(2)}) async-start(bf16[32,24,384]{2,1,0:T(8,128)(2,1)} %bitcast.15), calls=%async_computation | async-start | bytes 1179648 | tf_op jit(solution)/shard_map/all_to_all | solution.py:385
  24.5 18.5 %up.1.part_ref = f32[3,384,16,128]{3,2,1,0:T(8,128)} custom-call(f32[3,384,16,128]{3,2,1,0:T(8,128)} %u_ref.3, f32[3,1,6144]{2,1,0:T(1,128)} %get-tuple-element.18.low_ref, f32[3,1,6144]{2,1,0:T(1,128)} %get-tuple-element.19.high_ref, f32[9,16,128]{2,1,0:T(8,128)} %get-tuple-element.20.left_ref), custom_call_target="tpu_custom_call" | custom-call | flops 47185920 | bytes 18874368 | tf_op jit(solution)/shard_map/up/pallas_call | solution.py:389
  43.0 0.0 copy-start.2
  43.0 0.0 all-to-all-done
  43.0 0.0 copy-start
  43.0 0.8 copy-done
  43.8 10.7 %particles.1 = (f32[3,64,128]{2,1,0:T(8,128)}, bf16[768,384]{1,0:T(8,128)(2,1)}) custom-call(s32[1]{0:T(128)S(6)} %copy.8.live_ref, s32[256,1]{1,0:T(8,128)} %get-tuple-element.16.slot_ref, bf16[768,384]{1,0:T(8,128)(2,1)} %bitcast.12, bf16[64,128,512]{2,1,0:T(8,128)(2,1)} %weight_ref.1, f32[3,64,128]{2,1,0:T(8,128)} %velocity_ref.1), custom_call_target="tpu_custom_call" | custom-call | flops 400000000 | bytes 8388608 | tf_op jit(solution)/shard_map/particles/pallas_call | solution.py:408
  54.5 5.8 %all-to-all-start.1 = ((bf16[32,24,384]{2,1,0:T(8,128)(2,1)}), bf16[32,24,384]{2,1,0:T(8,128)(2,1)S(1)}, u32[]{:S(2)}, u32[]{:S(2)}) async-start(bf16[32,24,384]{2,1,0:T(8,128)(2,1)} %bitcast.14), calls=%async_computation.1 | async-start | bytes 1179648 | tf_op jit(solution)/shard_map/all_to_all | solution.py:432
  60.4 0.0 copy-done.2
  60.4 0.7 reshape_squeeze.3.index_ref
  61.1 13.4 %down.1 = f32[3,384,16,128]{3,2,1,0:T(8,128)} custom-call(f32[3,384,16,128]{3,2,1,0:T(8,128)} %u_ref.3, f32[3,384,16,128]{3,2,1,0:T(8,128)} %up.1.part_ref, f32[9,16,128]{2,1,0:T(8,128)} %get-tuple-element.25.right_ref), custom_call_target="tpu_custom_call" | custom-call | flops 47185920 | bytes 28311552 | tf_op jit(solution)/shard_map/down/pallas_call | solution.py:433
  74.5 2.6 %all-to-all-done.1 = bf16[32,24,384]{2,1,0:T(8,128)(2,1)S(1)} async-done(((bf16[32,24,384]{2,1,0:T(8,128)(2,1)}), bf16[32,24,384]{2,1,0:T(8,128)(2,1)S(1)}, u32[]{:S(2)}, u32[]{:S(2)}) %all-to-all-start.1) | async-done | bytes 589856 | tf_op jit(solution)/shard_map/all_to_all | solution.py:432
  77.1 0.0 copy-start.1
  77.1 0.8 copy-done.1
  77.9 13.6 %feedback.1 = f32[3,6144,128]{2,1,0:T(8,128)} custom-call(s32[1,768]{1,0:T(1,128)} %reshape_squeeze.3.index_ref, f32[3,6144,128]{2,1,0:T(8,128)} %bitcast.10, bf16[768,384]{1,0:T(8,128)(2,1)} %bitcast.13), custom_call_target="tpu_custom_call" | custom-call | flops 3623878656 | bytes 18874368 | tf_op jit(solution)/shard_map/feedback/pallas_call | solution.py:450
  (1 shorter events, 0.0 us)
Async XLA Ops:
  19.2 23.8 %all-to-all-start = ((bf16[32,24,384]{2,1,0:T(8,128)(2,1)}), bf16[32,24,384]{2,1,0:T(8,128)(2,1)S(1)}, u32[]{:S(2)}, u32[]{:S(2)}) async-start(bf16[32,24,384]{2,1,0:T(8,128)(2,1)} %bitcast.15), calls=%async_computation | async-start | bytes 1179648 | tf_op jit(solution)/shard_map/all_to_all | solution.py:385
  43.0 17.4 %copy-start.2 = (s32[32,1,128]{2,1,0:T(1,128)S(1)}, s32[32,1,128]{2,1,0:T(1,128)}, u32[]{:S(2)}) copy-start(s32[32,1,128]{2,1,0:T(1,128)} %get-tuple-element.15) | copy-start | bytes 49156
  43.0 0.8 copy-start
  54.5 22.6 %all-to-all-start.1 = ((bf16[32,24,384]{2,1,0:T(8,128)(2,1)}), bf16[32,24,384]{2,1,0:T(8,128)(2,1)S(1)}, u32[]{:S(2)}, u32[]{:S(2)}) async-start(bf16[32,24,384]{2,1,0:T(8,128)(2,1)} %bitcast.14), calls=%async_computation.1 | async-start | bytes 1179648 | tf_op jit(solution)/shard_map/all_to_all | solution.py:432
  77.1 0.8 copy-start.1

commit v2 on v1

--- a/solution.py
+++ b/solution.py
@@ -64,9 +64,10 @@
 
 def exchange_kernel(
     sizes, owner_ref, index_ref, field_hbm,
-    tile_ref, slot_ref, got_ref, low_ref, high_ref, left_ref, right_ref,
-    field_ref, table_ref, send_ref, got_smem, rows_ref, my_low, my_high, my_left, my_right,
-    field_sem, smem_sem, send_sem, recv_sem, edge_send, edge_recv,
+    reply_ref, slot_ref, got_ref, right_ref, part_hbm,
+    field_ref, table_ref, send_ref, got_smem, rows_ref, tile_ref, my_low, my_high, my_left, my_right,
+    low_ref, high_ref, left_ref, halo_ref, part_ref,
+    field_sem, smem_sem, send_sem, recv_sem, tile_send, tile_recv, edge_send, edge_recv, part_sem,
 ):
     gx, gz, kt, capacity, window = sizes
     devices = gx * gz
@@ -114,6 +115,44 @@
     got_ref[me] = send_ref[me]
     fetch.wait()
 
+    def arrive(d, carry):
+        parcel(d).wait()
+        return carry
+
+    lax.fori_loop(1, devices, arrive, 0)
+    copy = pltpu.make_async_copy(got_ref, got_smem, smem_sem)
+    copy.start()
+    copy.wait()
+
+    def collect(peer):
+        for k in range(capacity):
+            row = jnp.minimum(jnp.maximum(got_smem[peer, 0, k], 0), lines - 1)
+            for c in range(3):
+                rows_ref[c, k : k + 1, :] = field_ref[c, pl.ds(row, 1), :]
+        return [rows_ref[c].astype(BF16) for c in range(3)]
+
+    def tiles(d):
+        peer = lax.rem(me + d, devices)
+        return pltpu.make_async_remote_copy(
+            src_ref=tile_ref.at[peer],
+            dst_ref=reply_ref.at[me],
+            send_sem=tile_send.at[d],
+            recv_sem=tile_recv.at[d],
+            device_id=(peer // gz, lax.rem(peer, gz)),
+            device_id_type=pl.DeviceIdType.MESH,
+        )
+
+    def gather(d, carry):
+        peer = lax.rem(me + d, devices)
+        for c, value in enumerate(collect(peer)):
+            tile_ref[peer, :, c * span : (c + 1) * span] = value
+        tiles(d).start()
+        return carry
+
+    lax.fori_loop(1, devices, gather, 0)
+    for c, value in enumerate(collect(me)):
+        reply_ref[me, :, c * span : (c + 1) * span] = value
+
     def edge(k, src, dst, peer):
         return pltpu.make_async_remote_copy(
             src_ref=src,
@@ -131,12 +170,14 @@
         edge(3, my_low, high_ref, (x, lax.rem(z + gz - 1, gz))),
     ]
 
+    def load(i):
+        at = pl.ds(pl.multiple_of(i * wall, wall), wall)
+        u = [field_ref[c, at, :] for c in range(3)]
+        return u + [u[0] * u[c] for c in range(3)]
+
     def moments(order):
         def one(i, state):
-            at = pl.ds(pl.multiple_of(order(i) * wall, wall), wall)
-            u = [field_ref[c, at, :] for c in range(3)]
-            fields = u + [u[0] * u[c] for c in range(3)]
-            return tuple(f + ROOT * s for f, s in zip(fields, state))
+            return tuple(f + ROOT * s for f, s in zip(load(order(i)), state))
 
         return lax.fori_loop(0, window, one, (jnp.zeros((wall, span), F32),) * 6, unroll=4)
 
@@ -145,32 +186,6 @@
     for c in range(3):
         my_right[6 + c] = field_ref[c, lines - wall :, :]
     edges[0].start()
-    for k, value in enumerate(moments(lambda i: window - 1 - i)):
-        my_left[k] = value
-    for c in range(3):
-        my_left[6 + c] = field_ref[c, :wall, :]
-    edges[1].start()
-
-    def arrive(d, carry):
-        parcel(d).wait()
-        return carry
-
-    lax.fori_loop(1, devices, arrive, 0)
-    copy = pltpu.make_async_copy(got_ref, got_smem, smem_sem)
-    copy.start()
-    copy.wait()
-
-    def gather(d, carry):
-        for k in range(capacity):
-            row = jnp.minimum(jnp.maximum(got_smem[d, 0, k], 0), lines - 1)
-            for c in range(3):
-                rows_ref[c, pl.ds(d * capacity + k, 1), :] = field_ref[c, pl.ds(row, 1), :]
-        return carry
-
-    lax.fori_loop(0, devices, gather, 0)
-    for c in range(3):
-        tile_ref[:, c * span : (c + 1) * span] = rows_ref[c].astype(BF16)
-
     pick = end_lanes(span).astype(BF16)
     for c in range(3):
         for n in range(slab // window):
@@ -180,8 +195,61 @@
             my_high[c, :, part] = lanes[1:2]
     edges[2].start()
     edges[3].start()
-    for copy in edges:
-        copy.wait()
+    for k, value in enumerate(moments(lambda i: window - 1 - i)):
+        my_left[k] = value
+    for c in range(3):
+        my_left[6 + c] = field_ref[c, :wall, :]
+    edges[1].start()
+    for k in (0, 2, 3):
+        edges[k].wait()
+
+    rows = halo_ref.shape[1] // wall
+    lane = iota((wall, span), 1)
+    shape = (8, rows * wall)
+    first, second = iota(shape, 0) == 0, iota(shape, 0) == 1
+
+    def leave(n):
+        at = pl.ds(pl.multiple_of(n * rows * wall, rows * wall), rows * wall)
+        return pltpu.make_async_copy(part_ref.at[:, at, :], part_hbm.at[:, at, :], part_sem.at[n])
+
+    def chunk(n, carry):
+        at = pl.ds(pl.multiple_of(n * rows * wall, rows * wall), rows * wall)
+        for c in range(3):
+            ends = jnp.where(first, low_ref[c, :, at], jnp.where(second, high_ref[c, :, at], 0.0))
+            halo_ref[c] = dot(ends.astype(BF16), pick, 0, 0)
+
+        def one(i, carry):
+            fields, sums, carry = advance(load(n * rows + i), carry)
+            here = pl.ds(pl.multiple_of((n * rows + i) * wall, wall), wall)
+            for c in range(3):
+                u = fields[c]
+                near = jnp.where(lane == 0, 0.0, pltpu.roll(u, 1, 1))
+                far = jnp.where(lane == span - 1, 0.0, pltpu.roll(u, span - 1, 1))
+                edge_part = halo_ref[c, pl.ds(pl.multiple_of(i * wall, wall), wall), :]
+                curve = near + far + edge_part - 2.0 * u
+                part_ref[c, here, :] = 0.5 * GAMMA * sums[c] + VISCOSITY * curve
+            return carry
+
+        carry = lax.fori_loop(0, rows, one, carry, unroll=4)
+        leave(n).start()
+        return carry
+
+    border = [left_ref[6 + c] for c in range(3)]
+    border = border + [border[0] * border[c] for c in range(3)]
+    lax.fori_loop(0, slab // rows, chunk, tuple(left_ref[k] for k in range(6)) + tuple(border))
+
+    def finish(n, carry):
+        leave(n).wait()
+        return carry
+
+    lax.fori_loop(0, slab // rows, finish, 0)
+    edges[1].wait()
+
+    def receive(d, carry):
+        tiles(d).wait()
+        return carry
+
+    lax.fori_loop(1, devices, receive, 0)
 
 
 def load_state(state_ref, edge_ref):
@@ -192,44 +260,14 @@
         state_ref[6 + k] = edge[k]
 
 
-def advance(u_ref, i, carry):
+def advance(fields, carry):
     state, before = carry[:6], carry[6:]
-    fields = row_fields(u_ref, i)
     parts = [EPS * f + s for f, s in zip(before, state)]
     sums = [parts[3 + c] + fields[0] * parts[c] for c in range(3)]
     moved = [f + ROOT * s for f, s in zip(fields, state)]
     return fields, sums, tuple(moved) + tuple(fields)
 
 
-def up_kernel(u_ref, low_ref, high_ref, left_ref, out_ref, state_ref, halo_ref):
-    rows, wall, span = u_ref.shape[1:]
-    lane = iota((wall, span), 1)
-
-    @pl.when(pl.program_id(0) == 0)
-    def _():
-        load_state(state_ref, left_ref)
-
-    shape = (8, rows * wall)
-    pick = end_lanes(span)
-    for c in range(3):
-        ends = jnp.where(iota(shape, 0) == 0, low_ref[c], jnp.where(iota(shape, 0) == 1, high_ref[c], 0.0))
-        halo_ref[c] = dot(ends, pick, 0, 0).reshape(rows, wall, span)
-
-    def one(i, carry):
-        fields, sums, carry = advance(u_ref, i, carry)
-        for c in range(3):
-            u = fields[c]
-            near = jnp.where(lane == 0, 0.0, pltpu.roll(u, 1, 1))
-            far = jnp.where(lane == span - 1, 0.0, pltpu.roll(u, span - 1, 1))
-            curve = near + far + halo_ref[c, i] - 2.0 * u
-            out_ref[c, i] = 0.5 * GAMMA * sums[c] + VISCOSITY * curve
-        return carry
-
-    end = lax.fori_loop(0, rows, one, tuple(state_ref[k] for k in range(12)), unroll=4)
-    for k in range(12):
-        state_ref[k] = end[k]
-
-
 def down_kernel(u_ref, part_ref, right_ref, out_ref, state_ref):
     rows = u_ref.shape[1]
 
@@ -239,7 +277,7 @@
 
     def one(n, carry):
         i = rows - 1 - n
-        _, sums, carry = advance(u_ref, i, carry)
+        _, sums, carry = advance(row_fields(u_ref, i), carry)
         for c in range(3):
             out_ref[c, i] = part_ref[c, i] - 0.5 * GAMMA * sums[c]
         return carry
@@ -270,8 +308,10 @@
     tiles = jnp.concatenate([own_ref[c, pl.ds(base, group), :] for c in range(3)], 0).astype(BF16)
     row = iota((3 * group, particles), 0) % group
     sampled = jnp.zeros((3 * group, particles), F32)
-    for b in range(group):
-        sampled = jnp.where(row == b, dot(tiles, weight_ref[b], 1, 1), sampled)
+    for b in range(0, group, 2):
+        both = dot(tiles, weight_ref[b : b + 2].reshape(2 * particles, cells), 1, 1)
+        sampled = jnp.where(row == b, both[:, :particles], sampled)
+        sampled = jnp.where(row == b + 1, both[:, particles:], sampled)
     velocity = velocity_ref[...].reshape(3 * group, particles)
     live = jnp.where(row + base < live_ref[0], 1.0, 0.0)
     drag = live * (sampled - velocity) * (1.0 / RELAX_TIME)
@@ -345,35 +385,44 @@
     window = WINDOW if slab % WINDOW == 0 else slab
     lines = slab * wall
     dma = pltpu.SemaphoreType.DMA
-    tile_data, slot_ids, got, from_low, from_high, from_left, from_right = pl.pallas_call(
+    rows = largest_divisor(slab, 48)
+    parts = slab // rows
+    replies, slot_ids, got, from_right, up_part = pl.pallas_call(
         functools.partial(exchange_kernel, (gx, gz, kt, capacity, window)),
         out_shape=(
-            shape((slots, 3 * span), BF16),
+            shape((devices, capacity, 3 * span), BF16),
             shape((requests, 1), jnp.int32),
             shape((devices, 1, 128), jnp.int32),
-            shape((3, 1, lines), F32),
-            shape((3, 1, lines), F32),
             shape((9, wall, span), F32),
-            shape((9, wall, span), F32),
+            shape((3, lines, span), F32),
         ),
         in_specs=[vmem(), vmem(), pl.BlockSpec(memory_space=pl.ANY)],
-        out_specs=(vmem(),) * 7,
+        out_specs=(vmem(),) * 4 + (pl.BlockSpec(memory_space=pl.ANY),),
         scratch_shapes=[
             pltpu.VMEM((3, lines, span), F32),
             pltpu.VMEM((devices, 128), jnp.int32),
             pltpu.VMEM((devices, 1, 128), jnp.int32),
             pltpu.SMEM((devices, 1, 128), jnp.int32),
-            pltpu.VMEM((3, slots, span), F32),
+            pltpu.VMEM((3, capacity, span), F32),
+            pltpu.VMEM((devices, capacity, 3 * span), BF16),
             pltpu.VMEM((3, 1, lines), F32),
             pltpu.VMEM((3, 1, lines), F32),
             pltpu.VMEM((9, wall, span), F32),
             pltpu.VMEM((9, wall, span), F32),
+            pltpu.VMEM((3, 1, lines), F32),
+            pltpu.VMEM((3, 1, lines), F32),
+            pltpu.VMEM((9, wall, span), F32),
+            pltpu.VMEM((3, rows * wall, span), F32),
+            pltpu.VMEM((3, lines, span), F32),
             dma,
             dma,
             dma((devices,)),
             dma((devices,)),
+            dma((devices,)),
+            dma((devices,)),
             dma((4,)),
             dma((4,)),
+            dma((parts,)),
         ],
         compiler_params=pltpu.CompilerParams(
             vmem_limit_bytes=VMEM_LIMIT, collective_id=0, has_side_effects=True
@@ -382,29 +431,10 @@
         name="exchange",
     )(tile_owner.reshape(1, requests), tile_index.reshape(1, requests), velocity_field.reshape(3, lines, span))
     got = got[:, 0, :capacity].reshape(1, slots)
-    replies = lax.all_to_all(tile_data, ("gx", "gz"), split_axis=0, concat_axis=0, tiled=True)
-
-    rows = largest_divisor(slab, 48)
-    parts = slab // rows
-    up_part = pl.pallas_call(
-        up_kernel,
-        grid=(parts,),
-        out_shape=shape(velocity_field.shape, F32),
-        in_specs=[
-            pl.BlockSpec((3, rows, wall, span), lambda i: (0, i, 0, 0)),
-            pl.BlockSpec((3, 1, rows * wall), lambda i: (0, 0, i)),
-            pl.BlockSpec((3, 1, rows * wall), lambda i: (0, 0, i)),
-            pl.BlockSpec((9, wall, span), lambda i: (0, 0, 0)),
-        ],
-        out_specs=pl.BlockSpec((3, rows, wall, span), lambda i: (0, i, 0, 0)),
-        scratch_shapes=[pltpu.VMEM((12, wall, span), F32), pltpu.VMEM((3, rows, wall, span), F32)],
-        compiler_params=params(),
-        cost_estimate=cost(velocity_field.size * 20, field_bytes * 2),
-        name="up",
-    )(velocity_field, from_low, from_high, from_left)
-    replies, up_part = lax.optimization_barrier((replies, up_part))
-
-    group = 8
+    replies = replies.reshape(slots, 3 * span)
+    up_part = up_part.reshape(velocity_field.shape)
+
+    group = 16 if blocks % 16 == 0 else 8
     moved, outgoing = pl.pallas_call(
         functools.partial(particle_kernel, kt),
         grid=(blocks // group,),
@@ -446,7 +476,7 @@
         name="down",
     )(velocity_field, up_part, from_right)
 
-    chunk = 512 if lines % 512 == 0 else lines
+    chunk = 2048 if lines % 2048 == 0 else lines
     result = pl.pallas_call(
         add_kernel,
         grid=(lines // chunk,),

time: 92.4 us -> 88 us (0.952)
  starting transfers between devices: 10.4 us -> 3.74 us
  Pallas kernels: 74.8 us -> 78.4 us
    pallas_call x1, Pallas kernels: 18.6 us -> 45.4 us  [shards(): pl.pallas_call(functools.partial(exchange_kernel, (gx, gz, kt, capacity,...]
    pallas_call x1 -> x0, Pallas kernels: 18.5 us -> none  [shards(): pl.pallas_call(up_kernel, grid=(parts,), out_shape=shape(velocity_field.s...]
    all_to_all x1 -> x0, starting transfers between devices: 4.61 us -> none  [shards(): lax.all_to_all(tile_data, ('gx', 'gz'), split_axis=0, concat_axis=0, tile...]
    pallas_call x1, Pallas kernels: 13.6 us -> 11 us  [shards(): pl.pallas_call(add_kernel, grid=(lines // chunk,), out_shape=shape((3, li...]
    pallas_call x1, Pallas kernels: 10.7 us -> 8.58 us  [shards(): pl.pallas_call(functools.partial(particle_kernel, kt), grid=(blocks // gr...]
    all_to_all x1, starting transfers between devices: 5.83 us -> 3.74 us  [shards(): lax.all_to_all(outgoing, ('gx', 'gz'), split_axis=0, concat_axis=0, tiled...]
  transfers between devices with their start and end apart: 2 -> 1, of which waited for: 1 -> 1; matrix products, arithmetic and copies ran while one was open for 1% -> 1% of each run, Pallas kernels for 35% -> 15%
where the time goes in v2:
time: 88 us; the launch traced here: 87.5 us
  Pallas kernels  78.4 us (89%)
  starting transfers between devices  3.74 us (4%)
  waiting for transfers between devices  2.56 us (3%)
  local copies, waits for them, and re-layouts  1.54 us (2%)
  between operations  1.32 us (2%)
    pallas_call x1, Pallas kernels, shards(): pl.pallas_call(functools.partial(exchange_kernel, (gx, gz, kt, capacity,...  45.4 us
    pallas_call x1, Pallas kernels, shards(): pl.pallas_call(down_kernel, grid=(parts,), out_shape=shape(velocity_field...  13.4 us
    pallas_call x1, Pallas kernels, shards(): pl.pallas_call(add_kernel, grid=(lines // chunk,), out_shape=shape((3, li...  11 us
    pallas_call x1, Pallas kernels, shards(): pl.pallas_call(functools.partial(particle_kernel, kt), grid=(blocks // gr...  8.58 us
    all_to_all x1, starting transfers between devices, shards(): lax.all_to_all(outgoing, ('gx', 'gz'), split_axis=0, concat_axis=0, tiled...  3.74 us
    all_to_all x1, waiting for transfers between devices, shards(): lax.all_to_all(outgoing, ('gx', 'gz'), split_axis=0, concat_axis=0, tiled...  2.56 us
  transfers between devices with their start and end apart: 1, of which 1 were waited for; matrix products, arithmetic and copies ran while one was open for 1% of the time, Pallas kernels for 15%

profile of v2, /device:TPU:0, one launch (start us, length us, event | category | flops | bytes accessed | tf_op | source)
XLA Modules:
  0.0 87.5 jit_solution(6141424395505423113)
XLA Ops:
  1.3 45.4 %exchange.1 = (bf16[32,24,384]{2,1,0:T(8,128)(2,1)}, s32[256,1]{1,0:T(8,128)}, s32[32,1,128]{2,1,0:T(1,128)}, f32[9,16,128]{2,1,0:T(8,128)}, f32[3,6144,128]{2,1,0:T(8,128)}) custom-call(s32[1,256]{1,0:T(1,128)} %bitcast.16, s32[1,256]{1,0:T(1,128)} %bitcast.17, f32[3,6144,128]{2,1,0:T(8,128)} %bitcast.10), custom_call_target="tpu_custom_call" | custom-call | flops 10000000 | bytes 9437184 | tf_op jit(solution)/shard_map/exchange/pallas_call | solution.py:390
  46.7 0.0 copy-start.1
  46.7 8.6 %particles.1 = (f32[3,64,128]{2,1,0:T(8,128)}, bf16[768,384]{1,0:T(8,128)(2,1)}) custom-call(s32[1]{0:T(128)S(6)} %copy.8.live_ref, s32[256,1]{1,0:T(8,128)} %get-tuple-element.12.slot_ref, bf16[768,384]{1,0:T(8,128)(2,1)} %bitcast.14, bf16[64,128,512]{2,1,0:T(8,128)(2,1)} %weight_ref.1, f32[3,64,128]{2,1,0:T(8,128)} %velocity_ref.1), custom_call_target="tpu_custom_call" | custom-call | flops 400000000 | bytes 8388608 | tf_op jit(solution)/shard_map/particles/pallas_call | solution.py:438
  55.3 3.7 %all-to-all-start = ((bf16[32,24,384]{2,1,0:T(8,128)(2,1)}), bf16[32,24,384]{2,1,0:T(8,128)(2,1)S(1)}, u32[]{:S(2)}, u32[]{:S(2)}) async-start(bf16[32,24,384]{2,1,0:T(8,128)(2,1)} %bitcast.15), calls=%async_computation | async-start | bytes 1179648 | tf_op jit(solution)/shard_map/all_to_all | solution.py:462
  59.0 0.0 copy-done.1
  59.1 0.7 reshape_squeeze.3.index_ref
  59.8 13.4 %down.1 = f32[3,384,16,128]{3,2,1,0:T(8,128)} custom-call(f32[3,384,16,128]{3,2,1,0:T(8,128)} %u_ref.1, f32[3,384,16,128]{3,2,1,0:T(8,128)} %bitcast.12, f32[9,16,128]{2,1,0:T(8,128)} %get-tuple-element.17.right_ref), custom_call_target="tpu_custom_call" | custom-call | flops 47185920 | bytes 28311552 | tf_op jit(solution)/shard_map/down/pallas_call | solution.py:463
  73.2 2.6 %all-to-all-done = bf16[32,24,384]{2,1,0:T(8,128)(2,1)S(1)} async-done(((bf16[32,24,384]{2,1,0:T(8,128)(2,1)}), bf16[32,24,384]{2,1,0:T(8,128)(2,1)S(1)}, u32[]{:S(2)}, u32[]{:S(2)}) %all-to-all-start) | async-done | bytes 589856 | tf_op jit(solution)/shard_map/all_to_all | solution.py:462
  75.7 0.0 copy-start
  75.8 0.8 copy-done
  76.6 11.0 %feedback.1 = f32[3,6144,128]{2,1,0:T(8,128)} custom-call(s32[1,768]{1,0:T(1,128)} %reshape_squeeze.3.index_ref, f32[3,6144,128]{2,1,0:T(8,128)} %bitcast.9, bf16[768,384]{1,0:T(8,128)(2,1)} %bitcast.13), custom_call_target="tpu_custom_call" | custom-call | flops 3623878656 | bytes 18874368 | tf_op jit(solution)/shard_map/feedback/pallas_call | solution.py:480
  (1 shorter events, 0.0 us)
Async XLA Ops:
  46.7 12.3 %copy-start.1 = (s32[32,1,128]{2,1,0:T(1,128)S(1)}, s32[32,1,128]{2,1,0:T(1,128)}, u32[]{:S(2)}) copy-start(s32[32,1,128]{2,1,0:T(1,128)} %get-tuple-element.11) | copy-start | bytes 49156
  55.3 20.5 %all-to-all-start = ((bf16[32,24,384]{2,1,0:T(8,128)(2,1)}), bf16[32,24,384]{2,1,0:T(8,128)(2,1)S(1)}, u32[]{:S(2)}, u32[]{:S(2)}) async-start(bf16[32,24,384]{2,1,0:T(8,128)(2,1)} %bitcast.15), calls=%async_computation | async-start | bytes 1179648 | tf_op jit(solution)/shard_map/all_to_all | solution.py:462
  75.7 0.8 copy-start

commit v3 on v2

--- a/solution.py
+++ b/solution.py
@@ -19,7 +19,7 @@
 WINDOW = 96
 F32 = jnp.float32
 BF16 = jnp.bfloat16
-VMEM_LIMIT = 56 * 1024 * 1024
+VMEM_LIMIT = 54 * 1024 * 1024
 
 
 def iota(shape, dim):
@@ -358,8 +358,8 @@
     return pl.BlockSpec(memory_space=pltpu.SMEM)
 
 
-def params():
-    return pltpu.CompilerParams(vmem_limit_bytes=VMEM_LIMIT)
+def params(mebibytes):
+    return pltpu.CompilerParams(vmem_limit_bytes=mebibytes * 1024 * 1024)
 
 
 def cost(flops, nbytes):
@@ -454,7 +454,7 @@
             pltpu.VMEM((3, blocks, cells), F32),
             pltpu.VMEM((requests, 3 * span), F32),
         ],
-        compiler_params=params(),
+        compiler_params=params(16),
         cost_estimate=cost(4e8, interp_weight.size * 2),
         name="particles",
     )(block_count, slot_ids, replies, interp_weight, particle_velocity)
@@ -471,12 +471,12 @@
         ],
         out_specs=pl.BlockSpec((3, rows, wall, span), lambda i: (0, parts - 1 - i, 0, 0)),
         scratch_shapes=[pltpu.VMEM((12, wall, span), F32)],
-        compiler_params=params(),
+        compiler_params=params(56),
         cost_estimate=cost(velocity_field.size * 20, field_bytes * 3),
         name="down",
     )(velocity_field, up_part, from_right)
 
-    chunk = 2048 if lines % 2048 == 0 else lines
+    chunk = 1024 if lines % 1024 == 0 else lines
     result = pl.pallas_call(
         add_kernel,
         grid=(lines // chunk,),
@@ -487,7 +487,7 @@
             pl.BlockSpec((slots, 3 * span), lambda i: (0, 0)),
         ],
         out_specs=pl.BlockSpec((3, chunk, span), lambda i: (0, i, 0)),
-        compiler_params=params(),
+        compiler_params=params(56),
         cost_estimate=cost(2.0 * lines * slots * 3 * span, field_bytes * 2),
         name="feedback",
     )(got, fluid.reshape(3, lines, span), returned)

time: 88 us -> 88.1 us (level)
  Pallas kernels: 78.4 us -> 76.3 us
  local copies, waits for them, and re-layouts: 1.54 us -> 3.5 us
    pallas_call x1, Pallas kernels: 8.58 us -> 6.28 us  [shards(): pl.pallas_call(functools.partial(particle_kernel, kt), grid=(blocks // gr...]
    unnamed x4 -> x12, local copies, waits for them, and re-layouts: 0.82 us -> 2.78 us
where the time goes in v3:
time: 88.1 us; the launch traced here: 87.6 us
  Pallas kernels  76.3 us (87%)
  starting transfers between devices  3.73 us (4%)
  local copies, waits for them, and re-layouts  3.5 us (4%)
  waiting for transfers between devices  2.55 us (3%)
  between operations  1.5 us (2%)
    pallas_call x1, Pallas kernels, shards(): pl.pallas_call(functools.partial(exchange_kernel, (gx, gz, kt, capacity,...  45.7 us
    pallas_call x1, Pallas kernels, shards(): pl.pallas_call(down_kernel, grid=(parts,), out_shape=shape(velocity_field...  13.4 us
    pallas_call x1, Pallas kernels, shards(): pl.pallas_call(add_kernel, grid=(lines // chunk,), out_shape=shape((3, li...  10.9 us
    pallas_call x1, Pallas kernels, shards(): pl.pallas_call(functools.partial(particle_kernel, kt), grid=(blocks // gr...  6.28 us
    all_to_all x1, starting transfers between devices, shards(): lax.all_to_all(outgoing, ('gx', 'gz'), split_axis=0, concat_axis=0, tiled...  3.73 us
    unnamed x12, local copies, waits for them, and re-layouts  2.78 us
    all_to_all x1, waiting for transfers between devices, shards(): lax.all_to_all(outgoing, ('gx', 'gz'), split_axis=0, concat_axis=0, tiled...  2.55 us
  transfers between devices with their start and end apart: 1, of which 1 were waited for; matrix products, arithmetic and copies ran while one was open for 1% of the time, Pallas kernels for 15%

profile of v3, /device:TPU:0, one launch (start us, length us, event | category | flops | bytes accessed | tf_op | source)
XLA Modules:
  0.0 87.6 jit_solution(6292204249176788122)
XLA Ops:
  0.6 0.0 copy-start.3
  0.6 0.0 copy-start
  1.4 45.7 %exchange.1 = (bf16[32,24,384]{2,1,0:T(8,128)(2,1)}, s32[256,1]{1,0:T(8,128)}, s32[32,1,128]{2,1,0:T(1,128)}, f32[9,16,128]{2,1,0:T(8,128)}, f32[3,6144,128]{2,1,0:T(8,128)}) custom-call(s32[1,256]{1,0:T(1,128)} %bitcast.15, s32[1,256]{1,0:T(1,128)} %bitcast.16, f32[3,6144,128]{2,1,0:T(8,128)} %bitcast.11), custom_call_target="tpu_custom_call" | custom-call | flops 10000000 | bytes 9437184 | tf_op jit(solution)/shard_map/exchange/pallas_call | solution.py:390
  47.2 0.0 copy-done.3
  47.2 0.0 copy-done
  47.2 0.0 copy-start.1
  47.2 1.1 %copy-done.1 = bf16[32,24,384]{2,1,0:T(8,128)(2,1)S(1)} copy-done((bf16[32,24,384]{2,1,0:T(8,128)(2,1)S(1)}, bf16[32,24,384]{2,1,0:T(8,128)(2,1)}, u32[]{:S(2)}) %copy-start.1) | copy-done | bytes 589848
  48.3 0.0 copy-start.2
  48.3 0.9 %copy-done.2 = s32[256,1]{1,0:T(8,128)S(1)} copy-done((s32[256,1]{1,0:T(8,128)S(1)}, s32[256,1]{1,0:T(8,128)}, u32[]{:S(2)}) %copy-start.2) | copy-done | bytes 1048
  49.2 0.0 copy-start.5
  49.2 6.3 %particles.1 = (f32[3,64,128]{2,1,0:T(8,128)}, bf16[768,384]{1,0:T(8,128)(2,1)}) custom-call(s32[1]{0:T(128)S(6)} %copy.8.live_ref, s32[256,1]{1,0:T(8,128)S(1)} %copy-done.2, bf16[768,384]{1,0:T(8,128)(2,1)S(1)} %bitcast.9, bf16[64,128,512]{2,1,0:T(8,128)(2,1)S(1)} %copy-done, f32[3,64,128]{2,1,0:T(8,128)S(1)} %copy-done.3), custom_call_target="tpu_custom_call" | custom-call | flops 400000000 | bytes 8388608 | tf_op jit(solution)/shard_map/particles/pallas_call | solution.py:438
  55.5 3.7 %all-to-all-start = ((bf16[32,24,384]{2,1,0:T(8,128)(2,1)}), bf16[32,24,384]{2,1,0:T(8,128)(2,1)S(1)}, u32[]{:S(2)}, u32[]{:S(2)}) async-start(bf16[32,24,384]{2,1,0:T(8,128)(2,1)} %bitcast.6), calls=%async_computation | async-start | bytes 1179648 | tf_op jit(solution)/shard_map/all_to_all | solution.py:462
  59.2 0.0 copy-done.5
  59.3 0.7 reshape_squeeze.3.index_ref
  59.9 13.4 %down.1 = f32[3,384,16,128]{3,2,1,0:T(8,128)} custom-call(f32[3,384,16,128]{3,2,1,0:T(8,128)} %u_ref.1, f32[3,384,16,128]{3,2,1,0:T(8,128)} %bitcast.13, f32[9,16,128]{2,1,0:T(8,128)} %get-tuple-element.17.right_ref), custom_call_target="tpu_custom_call" | custom-call | flops 47185920 | bytes 28311552 | tf_op jit(solution)/shard_map/down/pallas_call | solution.py:463
  73.4 2.6 %all-to-all-done = bf16[32,24,384]{2,1,0:T(8,128)(2,1)S(1)} async-done(((bf16[32,24,384]{2,1,0:T(8,128)(2,1)}), bf16[32,24,384]{2,1,0:T(8,128)(2,1)S(1)}, u32[]{:S(2)}, u32[]{:S(2)}) %all-to-all-start) | async-done | bytes 589856 | tf_op jit(solution)/shard_map/all_to_all | solution.py:462
  75.9 0.0 copy-start.4
  75.9 0.8 copy-done.4
  76.7 10.9 %feedback.1 = f32[3,6144,128]{2,1,0:T(8,128)} custom-call(s32[1,768]{1,0:T(1,128)} %reshape_squeeze.3.index_ref, f32[3,6144,128]{2,1,0:T(8,128)} %bitcast.10, bf16[768,384]{1,0:T(8,128)(2,1)} %bitcast.14), custom_call_target="tpu_custom_call" | custom-call | flops 3623878656 | bytes 18874368 | tf_op jit(solution)/shard_map/feedback/pallas_call | solution.py:480
  (1 shorter events, 0.0 us)
Async XLA Ops:
  0.6 46.6 %copy-start.3 = (f32[3,64,128]{2,1,0:T(8,128)S(1)}, f32[3,64,128]{2,1,0:T(8,128)}, u32[]{:S(2)}) copy-start(f32[3,64,128]{2,1,0:T(8,128)} %velocity_ref.1) | copy-start | bytes 294916
  0.6 46.6 %copy-start = (bf16[64,128,512]{2,1,0:T(8,128)(2,1)S(1)}, bf16[64,128,512]{2,1,0:T(8,128)(2,1)}, u32[]{:S(2)}) copy-start(bf16[64,128,512]{2,1,0:T(8,128)(2,1)} %weight_ref.1) | copy-start | bytes 25165828
  47.2 1.1 %copy-start.1 = (bf16[32,24,384]{2,1,0:T(8,128)(2,1)S(1)}, bf16[32,24,384]{2,1,0:T(8,128)(2,1)}, u32[]{:S(2)}) copy-start(bf16[32,24,384]{2,1,0:T(8,128)(2,1)} %get-tuple-element.13) | copy-start | bytes 1769476
  48.3 0.9 %copy-start.2 = (s32[256,1]{1,0:T(8,128)S(1)}, s32[256,1]{1,0:T(8,128)}, u32[]{:S(2)}) copy-start(s32[256,1]{1,0:T(8,128)} %get-tuple-element.12.slot_ref) | copy-start | bytes 3076
  49.2 10.0 %copy-start.5 = (s32[32,1,128]{2,1,0:T(1,128)S(1)}, s32[32,1,128]{2,1,0:T(1,128)}, u32[]{:S(2)}) copy-start(s32[32,1,128]{2,1,0:T(1,128)} %get-tuple-element.11) | copy-start | bytes 49156
  55.5 20.5 %all-to-all-start = ((bf16[32,24,384]{2,1,0:T(8,128)(2,1)}), bf16[32,24,384]{2,1,0:T(8,128)(2,1)S(1)}, u32[]{:S(2)}, u32[]{:S(2)}) async-start(bf16[32,24,384]{2,1,0:T(8,128)(2,1)} %bitcast.6), calls=%async_computation | async-start | bytes 1179648 | tf_op jit(solution)/shard_map/all_to_all | solution.py:462
  75.9 0.8 copy-start.4
